TPU v7x, 256 devices: a whole 4x4x8 slice. The times are simulated.
256 devices in a mesh: freq: 4 (over x), row: 32 (over z, y), col: 2 (over core).
Axes of the slice: x: 4, y: 4, z: 8, core: 2. Of those that a mesh axis runs over, the one named last changes fastest.
Arguments:
- spectra: bfloat16 [2048, 4, 128, 128], P(('row', 'col'), 'freq'), may hold values from -56 to 56
- basis: bfloat16 [128, 64], replicated, may hold values from -0.5 to 0.5
- start_vectors: bfloat16 [8192, 8, 128], P(('row', 'col'), 'freq'), may hold values from -128 to 128
- pattern: int32 [64, 32, 2, 1], P('row', None, 'col'), may hold values from 0 to 1, as said below
Outputs:
- vectors: bfloat16 [8192, 8, 128], P(('row', 'col'), 'freq')
- affinity: float32 [64, 32, 2, 1, 128, 128], P('row', None, 'col', None, 'freq')
Inputs may be any that keep to these rules, and one draw needn't show every extreme that they name: `pattern`: every block is kept with itself. In each block row at most 12 blocks of each column set c are kept; every block row of one group of 2 consecutive block rows keeps exactly 12 in every column set, so the tile of block rows r * 2 to r * 2 + 1 and column set c holds at most 24 kept blocks, and some tile holds exactly 24.
All inputs are finite; a program needn't handle non-finite values.
Results may differ from a plain program's by a relative error of at most 0.015.
Values may be sent and summed in bfloat16 or wider, within the bound.
No kernel may reach another device: no remote copies, remote signals or barrier semaphores. Data moves between devices by JAX's collectives and lax.ppermute only.
A program may use at most 64 MiB of HBM per device.

v0:
```python
import math

import jax
import jax.numpy as jnp
from jax import lax
from jax.sharding import Mesh
from jax.sharding import PartitionSpec as P

ANG = 128
COMP = 64
COLS = 64
BLK = 128
FREQ_DEV = 2
IMG_DEV = 32
ITERS = 2
ROW = ("row_0", "row_1")
ROW_COL = ("row_0", "row_1", "col")


def in_order(pieces, dim):
    pieces = jnp.moveaxis(pieces, 0, dim)
    dims = pieces.shape
    return pieces.reshape(*dims[:dim], dims[dim] * dims[dim + 1], *dims[dim + 2 :])


def from_everyone(array, axis):
    copies = jnp.broadcast_to(array, (lax.axis_size(axis), *array.shape))
    return lax.all_to_all(copies, axis, split_axis=0, concat_axis=0, tiled=True)


def gather_directly(array, axis, dim):
    return in_order(from_everyone(array, axis), dim)


def gathered_by_axis(array, axes, dim):
    for axis in reversed(axes):
        array = lax.all_gather(array, axis, axis=dim, tiled=True)
    return array


def of_everyone(array, axis):
    return from_everyone(array, axis).sum(axis=0)


def in_blocks(array, dim, devices):
    before, after = (array.shape[:dim], array.shape[dim + 1 :])
    return jnp.moveaxis(array.reshape(*before, devices, -1, *after), dim, 0)


def sent_and_summed(array, axis, dim):
    devices = lax.axis_size(axis)
    pieces = lax.all_to_all(in_blocks(array, dim, devices), axis, 0, 0, tiled=True)
    return jnp.sum(pieces.astype(jnp.float32), axis=0)


def sent_together(arrays, axis, dim, along):
    widths = [math.prod(a.shape[along:]) for a in arrays]
    both = jnp.concatenate(
        [a.reshape(*a.shape[:along], w) for a, w in zip(arrays, widths)], axis=along
    )
    filled = sent_and_summed(both, axis, dim)
    pieces = jnp.split(filled, [sum(widths[:k]) for k in range(1, len(widths))], axis=along)
    return tuple(
        (b.reshape(*filled.shape[:along], *a.shape[along:]) for a, b in zip(arrays, pieces))
    )


def make_table(angles, freq_count):
    angle_ids = jnp.arange(angles, dtype=jnp.int32)
    orders = jnp.arange(freq_count, dtype=jnp.int32) + 1
    phase_steps = angle_ids[:, None] * orders[None, :] % angles
    phase_angle = phase_steps.astype(jnp.float32) * (2.0 * math.pi / angles)
    table_scale = 1.0 / math.sqrt(angles)
    return jnp.stack(
        [jnp.cos(phase_angle) * table_scale, -jnp.sin(phase_angle) * table_scale], axis=1
    ).astype(jnp.bfloat16)


def swap_halves(blocks):
    half_len = blocks.shape[-1] // 2
    return jnp.concatenate([-blocks[..., half_len:], blocks[..., :half_len]], axis=-1)


def pair_products(left_rows, right_rows):
    contract_dims = (((2,), (2,)), ((0,), (0,)))
    real_part = lax.dot_general(
        left_rows, right_rows, contract_dims, preferred_element_type=jnp.float32
    )
    imag_part = lax.dot_general(
        left_rows, swap_halves(right_rows), contract_dims, preferred_element_type=jnp.float32
    )
    return (real_part, imag_part)


def body(spectra, basis, start_vectors, pattern):
    group_devices = lax.axis_size("freq")
    row_devices = lax.axis_size(ROW)
    col_devices = lax.axis_size("col")
    freq_total = FREQ_DEV * group_devices
    dft_table = make_table(ANG, freq_total)
    angular = lax.dot_general(
        dft_table, spectra[:, 0], (((0,), (1,)), ((), ())), preferred_element_type=jnp.float32
    ).astype(jnp.bfloat16)
    radial = lax.dot_general(
        angular, basis, (((3,), (0,)), ((), ())), preferred_element_type=jnp.float32
    ).astype(jnp.bfloat16)
    coef_local = jnp.transpose(radial, (2, 1, 0, 3)).reshape(IMG_DEV, 1, freq_total, 2 * COMP)
    regrouped = lax.all_to_all(coef_local, "freq", split_axis=2, concat_axis=1, tiled=True)
    segment_len = IMG_DEV * group_devices
    own_coefs = regrouped.reshape(segment_len, FREQ_DEV, 2 * COMP)
    row_coefs = gather_directly(own_coefs, "col", 0)
    col_coefs = gathered_by_axis(own_coefs, ROW, 0)
    tile_rows = pattern.shape[0]
    seg_blocks = segment_len // BLK
    tile_cols = row_devices * seg_blocks
    most_row = max(2, tile_cols * 3 // 8)
    capacity = tile_rows * most_row
    group_len = 2 * most_row
    group_count = tile_rows // 2
    image_total = segment_len * row_devices * col_devices
    flat_mask = pattern.reshape(tile_rows * tile_cols)
    slot_order = jnp.argsort(1 - flat_mask, stable=True)[:capacity]
    slot_live = flat_mask[slot_order].astype(jnp.float32)
    slot_rows = slot_order // tile_cols
    slot_cols = slot_order % tile_cols
    grouped = (
        slot_rows.reshape(group_count, group_len),
        slot_cols.reshape(group_count, group_len),
        slot_live.reshape(group_count, group_len),
    )
    row_blocks = row_coefs.reshape(tile_rows, BLK, FREQ_DEV, 2 * COMP)
    col_blocks = col_coefs.reshape(tile_cols, BLK, FREQ_DEV, 2 * COMP)
    row_ids = jnp.arange(tile_rows, dtype=jnp.int32)

    def gather_cols(vectors_now):
        return gathered_by_axis(vectors_now, ROW, 0).reshape(tile_cols, BLK, FREQ_DEV, 2 * COLS)

    vectors = start_vectors
    degree = jnp.ones((segment_len, FREQ_DEV), jnp.float32)
    stored_kernels = None
    for step_idx in range(ITERS):
        vector_blocks = gather_cols(vectors)
        first_pass = stored_kernels is None

        def add_group(totals, pieces):
            row_sum, power_sum = totals
            if first_pass:
                group_rows, group_cols, group_live = pieces
            else:
                (group_rows, group_cols, group_live), kernel_all = pieces
            onehot = (row_ids[:, None] == group_rows[None, :]).astype(jnp.float32)
            vector_all = vector_blocks[group_cols]
            live_slots = group_live[:, None, None]
            if first_pass:
                left_all = row_blocks[group_rows]
                right_all = col_blocks[group_cols]
            freq_products = []
            freq_powers = []
            freq_kernels = []
            for freq_idx in range(FREQ_DEV):
                if first_pass:
                    cross_re, cross_im = pair_products(
                        left_all[:, :, freq_idx], right_all[:, :, freq_idx]
                    )
                    cross_re = cross_re / COMP
                    cross_im = cross_im / COMP
                    kernel = jnp.concatenate(
                        [
                            (cross_re * cross_re - cross_im * cross_im) * live_slots,
                            2.0 * cross_re * cross_im * live_slots,
                        ],
                        axis=-1,
                    ).astype(jnp.bfloat16)
                    freq_kernels.append(kernel)
                    magnitude = cross_re * cross_re + cross_im * cross_im
                    freq_powers.append(jnp.sum(magnitude * magnitude * live_slots, axis=2))
                else:
                    kernel = kernel_all[:, freq_idx]
                freq_vecs = vector_all[:, :, freq_idx]
                stacked = jnp.concatenate([freq_vecs, swap_halves(freq_vecs)], axis=1)
                freq_products.append(
                    lax.dot_general(
                        kernel,
                        stacked,
                        (((2,), (1,)), ((0,), (0,))),
                        preferred_element_type=jnp.float32,
                    )
                )
            product_all = jnp.stack(freq_products, axis=2)
            row_sum = row_sum + jnp.dot(onehot, product_all.reshape(group_len, -1)).reshape(
                row_sum.shape
            )
            if first_pass:
                power_all = jnp.stack(freq_powers, axis=2)
                power_sum = power_sum + jnp.dot(onehot, power_all.reshape(group_len, -1)).reshape(
                    power_sum.shape
                )
                return ((row_sum, power_sum), jnp.stack(freq_kernels, axis=1))
            return ((row_sum, power_sum), None)

        start_sums = (
            jnp.zeros((tile_rows, BLK, FREQ_DEV, 2 * COLS), jnp.float32),
            jnp.zeros((tile_rows, BLK, FREQ_DEV), jnp.float32),
        )
        scan_inputs = grouped if first_pass else (grouped, stored_kernels)
        final_sums, made_kernels = lax.scan(add_group, start_sums, scan_inputs)
        row_sum, power_sum, made_kernels = (
            final_sums[0].reshape(tile_rows * BLK, FREQ_DEV, 2 * COLS),
            final_sums[1].reshape(tile_rows * BLK, FREQ_DEV),
            made_kernels,
        )
        if step_idx == 0:
            stored_kernels = made_kernels
            summed, power_total = sent_together(
                (row_sum.astype(jnp.bfloat16), power_sum.astype(jnp.bfloat16)), "col", 0, 2
            )
            degree = jnp.sqrt(power_total)
        else:
            summed = sent_and_summed(row_sum.astype(jnp.bfloat16), "col", 0)
        scaled = summed / degree[..., None]
        squares = scaled[..., :COLS] * scaled[..., :COLS] + scaled[..., COLS:] * scaled[..., COLS:]
        col_sums = of_everyone(jnp.sum(squares, axis=0), ROW_COL)
        factor = lax.rsqrt(col_sums / image_total + 1e-06)
        vectors = (scaled * jnp.concatenate([factor, factor], axis=-1)[None]).astype(jnp.bfloat16)
    row_vecs = gather_directly(vectors, "col", 0).reshape(tile_rows, BLK, FREQ_DEV, 2 * COLS)
    col_final = gather_cols(vectors)
    part_rows = row_vecs.shape[1]

    def one_group(unused_carry, pieces):
        group_rows, group_cols, group_live = pieces
        left_all = row_vecs[group_rows]
        right_all = col_final[group_cols]
        power_total = jnp.zeros((group_len, part_rows, BLK), jnp.float32)
        for freq_idx in range(FREQ_DEV):
            gram_re, gram_im = pair_products(left_all[:, :, freq_idx], right_all[:, :, freq_idx])
            power_total = power_total + gram_re * gram_re + gram_im * gram_im
        return (unused_carry, power_total * (group_live[:, None, None] / COLS))

    unused_final, stacked = lax.scan(one_group, jnp.zeros((), jnp.float32), grouped)
    quarter = sent_and_summed(
        jnp.transpose(stacked.reshape(capacity, part_rows, BLK), (1, 0, 2)).astype(jnp.bfloat16),
        "freq",
        0,
    )
    scaled_terms = quarter * (1.0 / freq_total)
    quarter_len = quarter.shape[0]
    dense_rows = (
        jnp.zeros((quarter_len, tile_rows * tile_cols, BLK), jnp.float32)
        .at[:, slot_order]
        .set(scaled_terms)
    )
    affinity = jnp.transpose(dense_rows, (1, 0, 2)).reshape(
        tile_rows, row_devices, 1, seg_blocks, quarter_len, BLK
    )
    return (vectors, affinity)


def solution(mesh):
    split = Mesh(
        mesh.devices.reshape(mesh.shape["freq"], 8, 4, mesh.shape["col"]),
        ("freq", "row_0", "row_1", "col"),
    )
    placed = (
        P(ROW_COL, "freq", None, None),
        P(),
        P(ROW_COL, "freq", None),
        P(ROW, None, "col", None),
    )
    return jax.shard_map(
        body,
        mesh=split,
        in_specs=placed,
        out_specs=(P(ROW_COL, "freq", None), P(ROW, None, "col", None, "freq", None)),
        check_vma=False,
    )
```

profile of v0, /device:TPU:8, one launch (start us, length us, event | category | flops | bytes accessed | tf_op | source)
XLA Modules:
  0.0 320.8 jit_solution(3499954743594782733)
XLA Ops:
  7.2 0.9 copy.313
  8.2 13.4 %all_gather.26 = bf16[512,2,128]{2,0,1:T(8,128)(2,1)} all-gather(bf16[128,2,128]{2,0,1:T(8,128)(2,1)S(1)} %copy.313), channel_id=1, replica_groups=mesh['freq'=4,'row_0'=8,'row_1'=4,'col'=2] {'row_1'}, dimensions={0}, use_global_device_ids=true | all-gather | bytes 327680 | tf_op jit(solution)/shard_map/all_gather | solution.py:37
  22.5 9.7 %all_to_all.44 = bf16[32,1,8,128]{3,0,1,2:T(8,128)(2,1)S(1)} all-to-all(bf16[32,1,8,128]{3,0,1,2:T(8,128)(2,1)S(1)} %reshape.313), channel_id=1, replica_groups=mesh['freq'=4,'row_0'=8,'row_1'=4,'col'=2] {'freq'}, dimensions={2} | all-to-all | bytes 131072 | tf_op jit(solution)/shard_map/all_to_all | solution.py:108
  32.2 13.3 %all_gather.24 = bf16[512,2,128]{2,1,0:T(2,128)(2,1)} all-gather(bf16[128,2,128]{2,1,0:T(2,128)(2,1)S(1)} %bitcast.139), channel_id=1, replica_groups=mesh['freq'=4,'row_0'=8,'row_1'=4,'col'=2] {'row_1'}, dimensions={0}, use_global_device_ids=true | all-gather | bytes 327680 | tf_op jit(solution)/shard_map/all_gather | solution.py:37
  45.6 0.5 broadcast.269
  46.1 0.7 reduce.3
  46.9 2.0 sort.17
  48.9 0.7 gather_fusion.2
  49.7 3.8 %all_to_all.45 = bf16[2,128,2,128]{3,1,2,0:T(8,128)(2,1)S(1)} all-to-all(bf16[2,128,2,128]{3,1,2,0:T(8,128)(2,1)S(1)} %broadcast_in_dim.43), channel_id=1, replica_groups=mesh['freq'=4,'row_0'=8,'row_1'=4,'col'=2] {'col'}, dimensions={0} | all-to-all | bytes 262144 | tf_op jit(solution)/shard_map/all_to_all | solution.py:28
  53.6 0.8 gather_fusion
  54.4 10.9 %all-gather.7.cloned.1.call-done = bf16[4096,2,128]{2,0,1:T(8,128)(2,1)} async-done(((bf16[512,2,128]{2,0,1:T(8,128)(2,1)}), bf16[4096,2,128]{2,0,1:T(8,128)(2,1)}) %all-gather.7.cloned.1.call-update) | async-done | bytes 2097168 | tf_op jit(solution)/shard_map/all_gather | solution.py:37
  65.3 3.2 %copy.314 = bf16[32,128,2,128]{3,1,2,0:T(8,128)(2,1)} copy(bf16[32,128,2,128]{3,1,0,2:T(8,128)(2,1)} %bitcast.134) | data formatting | bytes 4194304 | tf_op jit(solution)/shard_map/reshape | solution.py:136
  68.5 2.4 gather_fusion.3
  71.1 0.9 copy-done.2
  72.2 2.3 slice_negate_fusion.4
  74.5 31.9 %all-gather.5.cloned.1.call-done = bf16[4096,2,128]{2,1,0:T(2,128)(2,1)} async-done(((bf16[512,2,128]{2,1,0:T(2,128)(2,1)}), bf16[4096,2,128]{2,1,0:T(2,128)(2,1)}) %all-gather.5.cloned.1.call-update) | async-done | bytes 2097168 | tf_op jit(solution)/shard_map/all_gather | solution.py:37
  106.4 3.5 %copy.311 = bf16[32,128,2,128]{3,1,2,0:T(8,128)(2,1)} copy(bf16[32,128,2,128]{3,2,1,0:T(2,128)(2,1)} %bitcast.135) | data formatting | bytes 4194304 | tf_op jit(solution)/shard_map/reshape | solution.py:132
  109.9 2.4 gather_fusion.1
  112.6 0.7 fusion.62
  113.2 0.7 fusion.61
  113.9 0.6 slice_negate_fusion.5
  114.5 0.7 convolution_multiply_fusion.4
  115.3 2.1 multiply_reduce_fusion.1
  117.5 1.0 fusion.37
  119.2 0.7 copy-done.7
  120.2 1.0 fusion.34
  121.3 1.6 copy.321
  123.0 1.2 reshape.229
  124.2 1.2 dot_general.87
  125.5 1.2 fusion.40
  127.4 0.8 copy.327
  128.2 3.8 %all_to_all.46 = bf16[2,128,2,129]{1,2,3,0:T(2,128)(2,1)S(1)} all-to-all(bf16[2,128,2,129]{1,2,3,0:T(2,128)(2,1)S(1)} %copy.327), channel_id=1, replica_groups=mesh['freq'=4,'row_0'=8,'row_1'=4,'col'=2] {'col'}, dimensions={0} | all-to-all | bytes 264192 | tf_op jit(solution)/shard_map/all_to_all | solution.py:52
  133.0 16.2 %all_to_all.47 = f32[64,1,128]{2,1,0:T(1,128)S(1)} all-to-all(f32[64,1,128]{2,1,0:T(1,128)S(1)} %reshape.323), channel_id=1, replica_groups=mesh['freq'=4,'row_0'=8,'row_1'=4,'col'=2] {'row_0','row_1','col'}, dimensions={0} | all-to-all | bytes 65536 | tf_op jit(solution)/shard_map/all_to_all | solution.py:28
  149.2 0.5 broadcast.273
  149.8 0.7 reduce.4
  151.0 12.3 %all_gather.28 = bf16[512,2,128]{2,1,0:T(2,128)(2,1)} all-gather(bf16[128,2,128]{2,1,0:T(2,128)(2,1)S(1)} %multiply_convert_fusion.6), channel_id=1, replica_groups=mesh['freq'=4,'row_0'=8,'row_1'=4,'col'=2] {'row_1'}, dimensions={0}, use_global_device_ids=true | all-gather | bytes 327680 | tf_op jit(solution)/shard_map/all_gather | solution.py:37
  163.3 37.7 %all-gather.9.cloned.1.call-done = bf16[4096,2,128]{2,1,0:T(2,128)(2,1)} async-done(((bf16[512,2,128]{2,1,0:T(2,128)(2,1)}), bf16[4096,2,128]{2,1,0:T(2,128)(2,1)}) %all-gather.9.cloned.1.call-update) | async-done | bytes 2097168 | tf_op jit(solution)/shard_map/all_gather | solution.py:37
  201.0 2.1 copy.333
  203.1 2.0 gather_fusion.4
  205.1 1.5 slice_bitcast_fusion.5
  207.3 0.8 copy-done.19
  208.3 1.0 fusion.31
  209.7 1.0 fusion.28
  210.9 1.6 copy.338
  212.5 1.2 reshape.232
  213.7 1.2 dot_general.95
  214.9 1.2 fusion.43
  216.2 3.8 %all_to_all.48 = bf16[2,128,2,128]{3,2,1,0:T(2,128)(2,1)S(1)} all-to-all(bf16[2,128,2,128]{3,2,1,0:T(2,128)(2,1)S(1)} %copy.340), channel_id=1, replica_groups=mesh['freq'=4,'row_0'=8,'row_1'=4,'col'=2] {'col'}, dimensions={0} | all-to-all | bytes 262144 | tf_op jit(solution)/shard_map/all_to_all | solution.py:52
  220.6 16.3 %all_to_all.49 = f32[64,1,128]{2,1,0:T(1,128)S(1)} all-to-all(f32[64,1,128]{2,1,0:T(1,128)S(1)} %reshape.325), channel_id=1, replica_groups=mesh['freq'=4,'row_0'=8,'row_1'=4,'col'=2] {'row_0','row_1','col'}, dimensions={0} | all-to-all | bytes 65536 | tf_op jit(solution)/shard_map/all_to_all | solution.py:28
  236.9 0.7 reduce.5
  238.1 12.3 %all_gather.30 = bf16[512,2,128]{2,1,0:T(2,128)(2,1)} all-gather(bf16[128,2,128]{2,1,0:T(2,128)(2,1)S(1)} %multiply_convert_fusion.5), channel_id=1, replica_groups=mesh['freq'=4,'row_0'=8,'row_1'=4,'col'=2] {'row_1'}, dimensions={0}, use_global_device_ids=true | all-gather | bytes 327680 | tf_op jit(solution)/shard_map/all_gather | solution.py:37
  250.5 4.1 %all_to_all.50 = bf16[2,128,2,128]{3,1,2,0:T(8,128)(2,1)S(1)} all-to-all(bf16[2,128,2,128]{3,1,2,0:T(8,128)(2,1)S(1)} %broadcast_in_dim.66), channel_id=1, replica_groups=mesh['freq'=4,'row_0'=8,'row_1'=4,'col'=2] {'col'}, dimensions={0} | all-to-all | bytes 262144 | tf_op jit(solution)/shard_map/all_to_all | solution.py:28
  254.5 0.8 gather_fusion.5
  255.4 32.7 %all-gather.11.cloned.1.call-done = bf16[4096,2,128]{2,1,0:T(2,128)(2,1)} async-done(((bf16[512,2,128]{2,1,0:T(2,128)(2,1)}), bf16[4096,2,128]{2,1,0:T(2,128)(2,1)}) %all-gather.11.cloned.1.call-update) | async-done | bytes 2097168 | tf_op jit(solution)/shard_map/all_gather | solution.py:37
  288.1 3.4 %copy.347 = bf16[32,128,2,128]{3,1,2,0:T(8,128)(2,1)} copy(bf16[32,128,2,128]{3,2,1,0:T(2,128)(2,1)} %bitcast.136) | data formatting | bytes 4194304 | tf_op jit(solution)/shard_map/reshape | solution.py:136
  291.6 2.4 gather_fusion.6
  294.1 0.3 slice_negate_fusion.1
  294.5 0.7 convolution_multiply_fusion.1
  295.5 0.7 convolution_multiply_fusion.2
  296.2 0.7 convolution_multiply_fusion
  297.0 0.7 multiply_convert_fusion
  297.7 13.5 %all_to_all.51 = bf16[4,32,24,128]{3,1,2,0:T(8,128)(2,1)S(1)} all-to-all(bf16[4,32,24,128]{3,1,2,0:T(8,128)(2,1)S(1)} %copy.351), channel_id=1, replica_groups=mesh['freq'=4,'row_0'=8,'row_1'=4,'col'=2] {'freq'}, dimensions={0} | all-to-all | bytes 1572864 | tf_op jit(solution)/shard_map/all_to_all | solution.py:52
  311.6 1.7 scatter_fusion
  313.3 1.0 copy-done.6
  (111 shorter events, 8.4 us)
Async XLA Ops:
  7.2 14.6 %copy-start = (bf16[32,1,128,128]{3,2,1,0:T(8,128)(2,1)S(1)}, bf16[32,1,128,128]{3,2,1,0:T(8,128)(2,1)}, u32[]{:S(2)}) copy-start(bf16[32,1,128,128]{3,2,1,0:T(8,128)(2,1)} %param.4) | copy-start | bytes 3145732
  7.2 14.8 %copy-start.12 = (bf16[128,64]{0,1:T(8,128)(2,1)S(1)}, bf16[128,64]{0,1:T(8,128)(2,1)}, u32[]{:S(2)}) copy-start(bf16[128,64]{0,1:T(8,128)(2,1)} %param.5) | copy-start | bytes 49156
  7.2 58.1 %all-gather.7.cloned.1.call-start = ((), (), s32[]{:S(2)}) async-start(), calls=%async_computation.9 | async-start | bytes 2359296 | tf_op jit(solution)/shard_map/all_gather | solution.py:37
  21.6 24.6 %copy-start.13 = (s32[2,32,1,1]{1,3,2,0:T(1,128)S(1)}, s32[2,32,1,1]{1,3,2,0:T(1,128)}, u32[]{:S(2)}) copy-start(s32[2,32,1,1]{1,3,2,0:T(1,128)} %param.7) | copy-start | bytes 772
  21.6 84.8 %all-gather.5.cloned.1.call-start = ((), (), s32[]{:S(2)}) async-start(), calls=%async_computation.8 | async-start | bytes 2359296 | tf_op jit(solution)/shard_map/all_gather | solution.py:37
  45.5 155.5 %all-gather.9.cloned.1.call-start = ((), (), s32[]{:S(2)}) async-start(), calls=%async_computation.10 | async-start | bytes 2359296 | tf_op jit(solution)/shard_map/all_gather | solution.py:37
  71.1 0.9 copy-start.2
  71.1 1.1 copy-start.4
  115.3 2.2 copy-start.5
  115.3 2.2 copy-start.9
  115.3 2.2 copy-start.10
  117.4 1.1 copy-start.18
  117.4 1.1 copy-start.20
  117.4 1.4 copy-start.14
  117.5 1.6 copy-start.16
  117.5 1.7 copy-start.3
  117.5 2.4 copy-start.7
  117.5 2.7 copy-start.8
  163.3 124.8 %all-gather.11.cloned.1.call-start = ((), (), s32[]{:S(2)}) async-start(), calls=%async_computation.11 | async-start | bytes 2359296 | tf_op jit(solution)/shard_map/all_gather | solution.py:37
  207.0 1.1 copy-start.19
  207.0 1.4 copy-start.21
  208.3 1.1 copy-start.15
  208.3 1.4 copy-start.17
  238.1 17.3 %copy-start.11 = (bf16[128,2,128]{2,1,0:T(2,128)(2,1)}, bf16[128,2,128]{2,1,0:T(2,128)(2,1)S(1)}, u32[]{:S(2)}) copy-start(bf16[128,2,128]{2,1,0:T(2,128)(2,1)S(1)} %multiply_convert_fusion.5) | copy-start | bytes 196612
  311.3 2.9 copy-start.1
  313.2 1.0 copy-start.6
Sparse Core Ops, SparseCore 0:
  21.7 43.5 all-gather.6
  67.1 39.3 all-gather.4
  163.4 37.5 all-gather.8
  250.5 37.5 all-gather.10
where the time goes:
time: 322 us; the launch traced here: 321 us
  blocking collectives  123 us (38%)
  waiting for transfers between devices  113 us (35%)
  local copies, waits for them, and re-layouts  45.3 us (14%)
  between operations  14.5 us (5%)
  matrix products  13.9 us (4%)
  other arithmetic  11.1 us (3%)
    all_gather x4, waiting for transfers between devices, gathered_by_axis(): array = lax.all_gather(array, axis, axis=dim, tiled=True)  113 us
    all_gather x4, blocking collectives, gathered_by_axis(): array = lax.all_gather(array, axis, axis=dim, tiled=True)  51.2 us
    all_to_all x4, blocking collectives, from_everyone(): return lax.all_to_all(copies, axis, split_axis=0, concat_axis=0, tiled=True)  40.4 us
    all_to_all x3, blocking collectives, sent_and_summed(): lax.all_to_all(in_blocks(array, dim, devices), axis, 0, 0, tiled=True)  21.2 us
    all_to_all x1, blocking collectives, body(): lax.all_to_all(coef_local, 'freq', split_axis=2, concat_axis=1, tiled=True)  9.72 us
    reshape x3, local copies, waits for them, and re-layouts, gather_cols(): gathered_by_axis(vectors_now, ROW, 0)  8.78 us
    unnamed x51, local copies, waits for them, and re-layouts  7.18 us
  transfers between devices with their start and end apart: 4, of which 4 were waited for; matrix products, arithmetic and copies ran while one was open for 5% of the time, Pallas kernels for 0%

commit v1 on v0

v1 whole, which is shorter than its diff:
```python
import math

import jax
import jax.numpy as jnp
from jax import lax
from jax.experimental import pallas as pl
from jax.experimental.pallas import tpu as pltpu
from jax.sharding import Mesh
from jax.sharding import PartitionSpec as P

ANG = 128
COMP = 64
COLS = 64
BLK = 128
FREQ_DEV = 2
IMG_DEV = 32
Z = 8
YC = 8
EXTRA = 16
MSG = FREQ_DEV * BLK + EXTRA
SPAN = Z * BLK
ROW = ("row_0", "row_1")
ROW_COL = ("row_0", "row_1", "col")
YCOL = ("row_1", "col")
F32 = jnp.float32
BF16 = jnp.bfloat16


def make_table(angles, freq_count):
    angle_ids = jnp.arange(angles, dtype=jnp.int32)
    orders = jnp.arange(freq_count, dtype=jnp.int32) + 1
    phase_steps = angle_ids[:, None] * orders[None, :] % angles
    phase_angle = phase_steps.astype(jnp.float32) * (2.0 * math.pi / angles)
    table_scale = 1.0 / math.sqrt(angles)
    return jnp.stack(
        [jnp.cos(phase_angle) * table_scale, -jnp.sin(phase_angle) * table_scale], axis=1
    ).astype(jnp.bfloat16)


def nt_dot(left, right):
    return lax.dot_general(
        left, right, (((1,), (1,)), ((), ())), preferred_element_type=jnp.float32
    )


def lane_signs(shape):
    lanes = lax.broadcasted_iota(jnp.int32, shape, len(shape) - 1)
    return jnp.where(lanes < COMP, -1.0, 1.0).astype(F32)


def swapped(block):
    wide = block.astype(F32)
    return (pltpu.roll(wide, COMP, 1) * lane_signs(wide.shape)).astype(BF16)


def swapped_back(block):
    wide = block.astype(F32)
    return (pltpu.roll(wide, COMP, 1) * -lane_signs(wide.shape)).astype(BF16)


def split_rows(rows):
    high = rows.astype(BF16)
    low = (rows - high.astype(F32)).astype(BF16)
    zeros = jnp.zeros((EXTRA - 4, BLK), BF16)
    return jnp.concatenate([high.astype(F32), low.astype(F32), zeros.astype(F32)], axis=0).astype(
        BF16
    )


def joined_rows(extra):
    total = jnp.sum(extra.astype(F32), axis=0)
    return total[0:2] + total[2:4]


def to_column(row):
    rows = lax.broadcasted_iota(jnp.int32, (BLK, BLK), 0)
    cols = lax.broadcasted_iota(jnp.int32, (BLK, BLK), 1)
    return jnp.sum(jnp.where(rows == cols, row, 0.0), axis=1, keepdims=True)


def load_stack(stack_ref, vec_ref, offset):
    for f in range(FREQ_DEV):
        for z in range(Z):
            block = vec_ref[z, offset + f * BLK : offset + (f + 1) * BLK, :]
            stack_ref[f, z * BLK : (z + 1) * BLK, :] = block
            stack_ref[f, SPAN + z * BLK : SPAN + (z + 1) * BLK, :] = swapped(block)


def mask_rows(mask_ref, which):
    extra = mask_ref[0].astype(F32)
    return jnp.where(which % 2 == 0, extra[0:Z], extra[Z : 2 * Z])


def cross_kernel(col_id, rows_ref, mask_ref, cols_ref, kern_ref, msg_ref, stack_ref):
    step = pl.program_id(0)

    @pl.when(step == 0)
    def _():
        load_stack(stack_ref, cols_ref, FREQ_DEV * BLK)

    masks = mask_rows(mask_ref, step)
    powers = []
    for f in range(FREQ_DEV):
        block = rows_ref[0, f * BLK : (f + 1) * BLK, :] * jnp.asarray(1.0 / COMP, BF16)
        left = jnp.concatenate([block, swapped_back(block)], axis=0)
        acc = jnp.zeros((BLK, BLK), F32)
        for z in range(Z):
            cross = nt_dot(left, cols_ref[z, f * BLK : (f + 1) * BLK, :])
            mask = masks[z : z + 1, :]
            re = cross[:BLK] * mask
            im = cross[BLK:] * mask
            re2 = re * re
            im2 = im * im
            kern_ref[0, f, :, z * BLK : (z + 1) * BLK] = (re2 - im2).astype(BF16)
            kern_ref[0, f, :, SPAN + z * BLK : SPAN + (z + 1) * BLK] = (2.0 * re * im).astype(BF16)
            mag = re2 + im2
            acc = acc + mag * mag
        high = acc.astype(BF16)
        low = (acc - high.astype(F32)).astype(BF16)
        ones = jnp.ones((EXTRA, BLK), BF16)
        powers.append((nt_dot(ones, high) + nt_dot(ones, low))[0:1])
        product = jnp.dot(kern_ref[0, f], stack_ref[f], preferred_element_type=F32)
        msg_ref[0, f * BLK : (f + 1) * BLK, :] = product.astype(BF16)
    msg_ref[0, FREQ_DEV * BLK :, :] = split_rows(jnp.concatenate(powers, axis=0))


def product_kernel(kern_ref, cols_ref, msg_ref, stack_ref, sums_ref):
    step = pl.program_id(0)

    @pl.when(step == 0)
    def _():
        load_stack(stack_ref, cols_ref, 0)
        sums_ref[...] = split_rows(group_sums(cols_ref))

    for f in range(FREQ_DEV):
        product = jnp.dot(kern_ref[0, f], stack_ref[f], preferred_element_type=F32)
        msg_ref[0, f * BLK : (f + 1) * BLK, :] = product.astype(BF16)
    msg_ref[0, FREQ_DEV * BLK :, :] = sums_ref[...]


def group_sums(cols_ref):
    rows = []
    for f in range(FREQ_DEV):
        acc = jnp.zeros((BLK, BLK), F32)
        for z in range(Z):
            block = cols_ref[z, f * BLK : (f + 1) * BLK, :].astype(F32)
            acc = acc + block * block
        rows.append(jnp.sum(acc, axis=0, keepdims=True))
    both = jnp.concatenate(rows + rows + rows + rows, axis=0)
    return (both + pltpu.roll(both, COLS, 1))[0:2]


def first_combine(recv_ref, out_ref, inverse_ref):
    powers = joined_rows(recv_ref[:, FREQ_DEV * BLK :, :])
    inverse = lax.rsqrt(powers)
    for f in range(FREQ_DEV):
        total = jnp.sum(recv_ref[:, f * BLK : (f + 1) * BLK, :].astype(F32), axis=0)
        column = jnp.broadcast_to(to_column(inverse[f : f + 1]), (BLK, BLK))
        inverse_ref[f * BLK : (f + 1) * BLK, :] = column
        value = (total * column).astype(BF16)
        for z in range(Z):
            out_ref[z, f * BLK : (f + 1) * BLK, :] = value


def second_combine(recv_ref, inverse_ref, scaled_ref, out_ref, *, images):
    means = joined_rows(recv_ref[:, FREQ_DEV * BLK :, :]) / images
    factor = lax.rsqrt(means + 1e-06)
    for f in range(FREQ_DEV):
        total = jnp.sum(recv_ref[:, f * BLK : (f + 1) * BLK, :].astype(F32), axis=0)
        value = total * inverse_ref[f * BLK : (f + 1) * BLK, :] * factor[f : f + 1]
        scaled_ref[f * BLK : (f + 1) * BLK, :] = value
        value = value.astype(BF16)
        for z in range(Z):
            out_ref[z, f * BLK : (f + 1) * BLK, :] = value


def sums_message(cols_ref, scaled_ref, out_ref):
    extra = split_rows(group_sums(cols_ref))
    value = scaled_ref[...].astype(BF16)
    for k in range(YC):
        out_ref[k, : FREQ_DEV * BLK, :] = value
        out_ref[k, FREQ_DEV * BLK :, :] = extra


def gram_kernel(
    col_id, rows_ref, mask_ref, sums_ref, cols_ref, scaled_ref, out_ref, vec_ref, *, images, freqs
):
    step = pl.program_id(0)
    means = joined_rows(sums_ref[...]) / images
    factor = lax.rsqrt(means + 1e-06)
    square = factor * factor

    @pl.when(step == 0)
    def _():
        for f in range(FREQ_DEV):
            vec_ref[f] = (scaled_ref[f * BLK : (f + 1) * BLK, :] * factor[f : f + 1]).astype(BF16)

    masks = mask_rows(mask_ref, step) * (1.0 / (COLS * freqs))
    lefts = []
    for f in range(FREQ_DEV):
        block = (rows_ref[0, f * BLK : (f + 1) * BLK, :].astype(F32) * square[f : f + 1]).astype(
            BF16
        )
        lefts.append(jnp.concatenate([block, swapped_back(block)], axis=0))
    for z in range(Z):
        total = jnp.zeros((BLK, BLK), F32)
        for f in range(FREQ_DEV):
            gram = nt_dot(lefts[f], cols_ref[z, f * BLK : (f + 1) * BLK, :])
            total = total + gram[:BLK] * gram[:BLK] + gram[BLK:] * gram[BLK:]
        value = (total * masks[z : z + 1, :]).astype(BF16)
        for x in range(4):
            out_ref[x, 0, z] = value[x * 32 : (x + 1) * 32]


def whole(shape):
    return pl.BlockSpec(shape, lambda *_: (0,) * len(shape))


def exchange(pieces, axes):
    return lax.all_to_all(pieces, axes, 0, 0, tiled=True)


def body(spectra, basis, start_vectors, pattern):
    group_devices = lax.axis_size("freq")
    images = BLK * lax.axis_size(ROW_COL)
    freq_total = FREQ_DEV * group_devices
    col_id = lax.axis_index("col").astype(jnp.int32).reshape(1)
    dft_table = make_table(ANG, freq_total)
    angular = lax.dot_general(
        dft_table, spectra[:, 0], (((0,), (1,)), ((), ())), preferred_element_type=jnp.float32
    ).astype(jnp.bfloat16)
    radial = lax.dot_general(
        angular, basis, (((3,), (0,)), ((), ())), preferred_element_type=jnp.float32
    ).astype(jnp.bfloat16)
    coef_local = jnp.transpose(radial, (1, 2, 0, 3)).reshape(
        group_devices, FREQ_DEV, IMG_DEV, 2 * COMP
    )
    regrouped = exchange(coef_local, "freq")
    own = jnp.transpose(regrouped, (1, 2, 0, 3)).reshape(FREQ_DEV * BLK, 2 * COMP)
    start = jnp.transpose(start_vectors, (1, 0, 2)).reshape(FREQ_DEV * BLK, 2 * COLS)
    to_z = jnp.concatenate([own, start], axis=0)
    cols = exchange(jnp.broadcast_to(to_z, (Z, *to_z.shape)), "row_0")
    kept = jnp.transpose(pattern.reshape(2, Z, YC // 2), (2, 0, 1)).reshape(YC // 2, 1, EXTRA, 1)
    kept = jnp.broadcast_to(kept.astype(BF16), (YC // 2, 2, EXTRA, BLK)).reshape(YC, EXTRA, BLK)
    to_yc = jnp.concatenate([jnp.broadcast_to(own, (YC, *own.shape)), kept], axis=1)
    rows = exchange(to_yc, YCOL)

    row_spec = pl.BlockSpec((1, FREQ_DEV * BLK, BLK), lambda i, c: (i, 0, 0))
    mask_spec = pl.BlockSpec((1, EXTRA, BLK), lambda i, c: (i // 2 * 2 + c[0], 16, 0))
    big = pltpu.CompilerParams(vmem_limit_bytes=48 << 20)
    stack = pltpu.VMEM((FREQ_DEV, 2 * SPAN, BLK), BF16)
    msg_shape = jax.ShapeDtypeStruct((YC, MSG, BLK), BF16)
    kernels, partial = pl.pallas_call(
        cross_kernel,
        grid_spec=pltpu.PrefetchScalarGridSpec(
            num_scalar_prefetch=1,
            grid=(YC,),
            in_specs=[row_spec, mask_spec, whole(cols.shape)],
            out_specs=[
                pl.BlockSpec((1, FREQ_DEV, BLK, 2 * SPAN), lambda i, c: (i, 0, 0, 0)),
                pl.BlockSpec((1, MSG, BLK), lambda i, c: (i, 0, 0)),
            ],
            scratch_shapes=[stack],
        ),
        out_shape=[jax.ShapeDtypeStruct((YC, FREQ_DEV, BLK, 2 * SPAN), BF16), msg_shape],
        compiler_params=big,
        name="cross",
    )(col_id, rows, rows, cols)
    got = exchange(partial, YCOL)
    own_shape = (FREQ_DEV * BLK, BLK)
    to_z, inverse = pl.pallas_call(
        first_combine,
        out_shape=[
            jax.ShapeDtypeStruct((Z, *own_shape), BF16),
            jax.ShapeDtypeStruct(own_shape, F32),
        ],
        name="combine_one",
    )(got)
    cols = exchange(to_z, "row_0")
    partial = pl.pallas_call(
        product_kernel,
        grid=(YC,),
        in_specs=[
            pl.BlockSpec((1, FREQ_DEV, BLK, 2 * SPAN), lambda i: (i, 0, 0, 0)),
            whole(cols.shape),
        ],
        out_specs=pl.BlockSpec((1, MSG, BLK), lambda i: (i, 0, 0)),
        out_shape=msg_shape,
        scratch_shapes=[stack, pltpu.VMEM((EXTRA, BLK), BF16)],
        compiler_params=big,
        name="product",
    )(kernels, cols)
    got = exchange(partial, YCOL)
    scaled, to_z = pl.pallas_call(
        lambda *refs: second_combine(*refs, images=images),
        out_shape=[
            jax.ShapeDtypeStruct(own_shape, F32),
            jax.ShapeDtypeStruct((Z, *own_shape), BF16),
        ],
        name="combine_two",
    )(got, inverse)
    cols = exchange(to_z, "row_0")
    to_yc = pl.pallas_call(sums_message, out_shape=msg_shape, name="sums")(cols, scaled)
    last_rows = exchange(to_yc, YCOL)
    tiles, vectors = pl.pallas_call(
        lambda *refs: gram_kernel(*refs, images=images, freqs=freq_total),
        grid_spec=pltpu.PrefetchScalarGridSpec(
            num_scalar_prefetch=1,
            grid=(YC,),
            in_specs=[
                row_spec,
                mask_spec,
                pl.BlockSpec((YC, EXTRA, BLK), lambda i, c: (0, 16, 0)),
                whole(cols.shape),
                whole(own_shape),
            ],
            out_specs=[
                pl.BlockSpec((4, 1, Z, 32, BLK), lambda i, c: (0, i, 0, 0, 0)),
                whole((FREQ_DEV, BLK, BLK)),
            ],
        ),
        out_shape=[
            jax.ShapeDtypeStruct((4, YC, Z, 32, BLK), BF16),
            jax.ShapeDtypeStruct((FREQ_DEV, BLK, BLK), BF16),
        ],
        compiler_params=big,
        name="gram",
    )(col_id, last_rows, rows, last_rows, cols, scaled)
    vectors = jnp.transpose(vectors, (1, 0, 2))
    arrived = exchange(tiles.reshape(16, 2, Z, 32, BLK), ("freq", "row_1"))
    summed = jnp.sum(arrived.reshape(4, 4, 2, Z, 32, BLK).astype(F32), axis=0)
    affinity = jnp.transpose(summed, (1, 2, 0, 3, 4)).reshape(2, 32, 1, 1, 32, BLK)
    return (vectors, affinity)


def solution(mesh):
    split = Mesh(
        mesh.devices.reshape(mesh.shape["freq"], 8, 4, mesh.shape["col"]),
        ("freq", "row_0", "row_1", "col"),
    )
    placed = (
        P(ROW_COL, "freq", None, None),
        P(),
        P(ROW_COL, "freq", None),
        P(ROW, None, "col", None),
    )
    return jax.shard_map(
        body,
        mesh=split,
        in_specs=placed,
        out_specs=(P(ROW_COL, "freq", None), P(ROW, None, "col", None, "freq", None)),
        check_vma=False,
    )
```

time: 322 us -> 223 us (0.69)
  waiting for transfers between devices: 113 us -> 71.8 us
  local copies, waits for them, and re-layouts: 45.3 us -> 6.54 us
  blocking collectives: 123 us -> 85.2 us
  Pallas kernels: 0 us -> 29.2 us
  starting transfers between devices: 0.16 us -> 23.3 us
  between operations: 14.5 us -> 0.75 us
  matrix products: 13.9 us -> 1.16 us
  other arithmetic: 11.1 us -> 3.72 us
    all_gather x4 -> x0, waiting for transfers between devices: 113 us -> none  [gathered_by_axis(): array = lax.all_gather(array, axis, axis=dim, tiled=True)]
    all_to_all x0 -> x4, waiting for transfers between devices: none -> 71.8 us  [exchange(): return lax.all_to_all(pieces, axes, 0, 0, tiled=True)]
    all_gather x4 -> x0, blocking collectives: 51.2 us -> none  [gathered_by_axis(): array = lax.all_gather(array, axis, axis=dim, tiled=True)]
    pallas_call x0 -> x6, Pallas kernels: none -> 29.2 us  [the longest x1 11.4 us: body(): pl.pallas_call(cross_kernel, grid_spec=pltpu.PrefetchScalarGridSpec(num_s...]
    all_to_all x0 -> x4, starting transfers between devices: none -> 23.3 us  [exchange(): return lax.all_to_all(pieces, axes, 0, 0, tiled=True)]
    reshape x11 -> x1, local copies, waits for them, and re-layouts: 15.2 us -> 0.75 us  [body(): jnp.transpose(radial, (1, 2, 0, 3))]
    all_to_all x8 -> x5, blocking collectives: 71.3 us -> 85.2 us  [exchange(): return lax.all_to_all(pieces, axes, 0, 0, tiled=True)]
    dot_general x15 -> x0, matrix products: 13.5 us -> none  [the longest x4 4.34 us: pair_products(): lax.dot_general(left_rows, swap_halves(right_rows), contract_dims, prefer...]
  transfers between devices with their start and end apart: 4 -> 4, of which waited for: 4 -> 4; matrix products, arithmetic and copies ran while one was open for 5% -> 1% of each run, Pallas kernels for 0% -> 0%
where the time goes in v1:
time: 223 us; the launch traced here: 222 us
  blocking collectives  85.2 us (38%)
  waiting for transfers between devices  71.8 us (32%)
  Pallas kernels  29.2 us (13%)
  starting transfers between devices  23.3 us (10%)
  local copies, waits for them, and re-layouts  6.54 us (3%)
  other arithmetic  3.72 us (2%)
    all_to_all x5, blocking collectives, exchange(): return lax.all_to_all(pieces, axes, 0, 0, tiled=True)  85.2 us
    all_to_all x4, waiting for transfers between devices, exchange(): return lax.all_to_all(pieces, axes, 0, 0, tiled=True)  71.8 us
    all_to_all x4, starting transfers between devices, exchange(): return lax.all_to_all(pieces, axes, 0, 0, tiled=True)  23.3 us
    pallas_call x1, Pallas kernels, body(): pl.pallas_call(cross_kernel, grid_spec=pltpu.PrefetchScalarGridSpec(num_s...  11.4 us
    pallas_call x1, Pallas kernels, body(): pl.pallas_call(product_kernel, grid=(YC,), in_specs=[pl.BlockSpec((1, FRE...  7.57 us
  transfers between devices with their start and end apart: 4, of which 4 were waited for; matrix products, arithmetic and copies ran while one was open for 1% of the time, Pallas kernels for 0%

profile of v1, /device:TPU:8, one launch (start us, length us, event | category | flops | bytes accessed | tf_op | source)
XLA Modules:
  0.0 221.7 jit_solution(1161247950392450246)
XLA Ops:
  0.6 0.0 copy-start
  0.7 0.1 multiply_convert_fusion.1
  0.8 1.1 copy-done
  1.9 0.2 convolution_convert_fusion
  2.1 0.0 copy-start.4
  2.1 0.9 fusion
  3.0 0.1 copy.25
  3.2 0.7 reshape.145
  3.9 4.3 %all-to-all-start = ((bf16[4,2,32,128]{3,2,1,0:T(8,128)(2,1)}), bf16[4,2,32,128]{3,2,1,0:T(8,128)(2,1)S(1)}, u32[]{:S(2)}, u32[]{:S(2)}) async-start(bf16[4,2,32,128]{3,2,1,0:T(8,128)(2,1)} %reshape.145), calls=%async_computation | async-start | bytes 131072 | tf_op jit(solution)/shard_map/all_to_all | solution.py:220
  8.2 0.7 convert_reduce_fusion.1
  8.9 0.1 convert_element_type.55
  9.0 0.1 copy.34
  9.1 4.7 %all-to-all-done = bf16[4,2,32,128]{3,2,1,0:T(8,128)(2,1)S(1)} async-done(((bf16[4,2,32,128]{3,2,1,0:T(8,128)(2,1)}), bf16[4,2,32,128]{3,2,1,0:T(8,128)(2,1)S(1)}, u32[]{:S(2)}, u32[]{:S(2)}) %all-to-all-start) | async-done | bytes 65568 | tf_op jit(solution)/shard_map/all_to_all | solution.py:220
  13.9 0.1 copy.26
  13.9 0.1 broadcast_in_dim.20
  14.0 0.1 broadcast_in_dim.17
  14.1 0.8 pad_maximum_fusion
  14.9 4.9 %all-to-all-start.1 = ((bf16[8,272,128]{2,1,0:T(8,128)(2,1)}), bf16[8,272,128]{2,1,0:T(8,128)(2,1)S(1)}, u32[]{:S(2)}, u32[]{:S(2)}) async-start(bf16[8,272,128]{2,1,0:T(8,128)(2,1)} %pad_maximum_fusion), calls=%async_computation.1 | async-start | bytes 1114112 | tf_op jit(solution)/shard_map/all_to_all | solution.py:220
  19.8 0.0 copy-done.4
  19.9 9.2 %all-to-all-done.1.rows_ref.mask_ref.refs_2_ = bf16[8,272,128]{2,1,0:T(8,128)(2,1)S(1)} async-done(((bf16[8,272,128]{2,1,0:T(8,128)(2,1)}), bf16[8,272,128]{2,1,0:T(8,128)(2,1)S(1)}, u32[]{:S(2)}, u32[]{:S(2)}) %all-to-all-start.1) | async-done | bytes 557088 | tf_op jit(solution)/shard_map/all_to_all | solution.py:220
  29.1 1.1 broadcast_in_dim.21
  30.2 8.5 %all-to-all-start.2 = ((bf16[8,512,128]{2,1,0:T(8,128)(2,1)}), bf16[8,512,128]{2,1,0:T(8,128)(2,1)S(1)}, u32[]{:S(2)}, u32[]{:S(2)}) async-start(bf16[8,512,128]{2,1,0:T(8,128)(2,1)} %broadcast_in_dim.21), calls=%async_computation.2 | async-start | bytes 2097152 | tf_op jit(solution)/shard_map/all_to_all | solution.py:220
  38.6 28.4 %all-to-all-done.2.cols_ref = bf16[8,512,128]{2,1,0:T(8,128)(2,1)S(1)} async-done(((bf16[8,512,128]{2,1,0:T(8,128)(2,1)}), bf16[8,512,128]{2,1,0:T(8,128)(2,1)S(1)}, u32[]{:S(2)}, u32[]{:S(2)}) %all-to-all-start.2) | async-done | bytes 1048608 | tf_op jit(solution)/shard_map/all_to_all | solution.py:220
  67.1 11.4 %cross.1 = (bf16[8,2,128,2048]{3,2,1,0:T(8,128)(2,1)}, bf16[8,272,128]{2,1,0:T(8,128)(2,1)S(1)}) custom-call(s32[1]{0:T(128)} %bitcast.col_id.refs_0_, bf16[8,272,128]{2,1,0:T(8,128)(2,1)S(1)} %all-to-all-done.1.rows_ref.mask_ref.refs_2_, bf16[8,272,128]{2,1,0:T(8,128)(2,1)S(1)} %all-to-all-done.1.rows_ref.mask_ref.refs_2_, ...), custom_call_target="tpu_custom_call" | custom-call | tf_op jit(solution)/shard_map/cross/pallas_call | solution.py:253
  78.5 13.8 %all_to_all.45.recv_ref = bf16[8,272,128]{2,1,0:T(8,128)(2,1)} all-to-all(bf16[8,272,128]{2,1,0:T(8,128)(2,1)S(1)} %get-tuple-element.11), channel_id=1, replica_groups=mesh['freq'=4,'row_0'=8,'row_1'=4,'col'=2] {'row_1','col'}, dimensions={0} | all-to-all | bytes 1114112 | tf_op jit(solution)/shard_map/all_to_all | solution.py:220
  92.3 2.0 combine_one.1
  94.3 21.3 %all_to_all.46.cols_ref = bf16[8,256,128]{2,1,0:T(8,128)(2,1)S(1)} all-to-all(bf16[8,256,128]{2,1,0:T(8,128)(2,1)} %get-tuple-element.12), channel_id=1, replica_groups=mesh['freq'=4,'row_0'=8,'row_1'=4,'col'=2] {'row_0'}, dimensions={0} | all-to-all | bytes 1048576 | tf_op jit(solution)/shard_map/all_to_all | solution.py:220
  115.6 7.6 %product.1 = bf16[8,272,128]{2,1,0:T(8,128)(2,1)S(1)} custom-call(bf16[8,2,128,2048]{3,2,1,0:T(8,128)(2,1)} %get-tuple-element.10.kern_ref, bf16[8,256,128]{2,1,0:T(8,128)(2,1)S(1)} %all_to_all.46.cols_ref), custom_call_target="tpu_custom_call" | custom-call | tf_op jit(solution)/shard_map/product/pallas_call | solution.py:280
  123.2 13.8 %all_to_all.47.refs_0_ = bf16[8,272,128]{2,1,0:T(8,128)(2,1)} all-to-all(bf16[8,272,128]{2,1,0:T(8,128)(2,1)S(1)} %product.1), channel_id=1, replica_groups=mesh['freq'=4,'row_0'=8,'row_1'=4,'col'=2] {'row_1','col'}, dimensions={0} | all-to-all | bytes 1114112 | tf_op jit(solution)/shard_map/all_to_all | solution.py:220
  137.0 2.0 combine_two.1
  139.0 0.0 copy-start.3
  139.0 22.1 %all_to_all.48.cols_ref.refs_4_ = bf16[8,256,128]{2,1,0:T(8,128)(2,1)} all-to-all(bf16[8,256,128]{2,1,0:T(8,128)(2,1)} %get-tuple-element.14), channel_id=1, replica_groups=mesh['freq'=4,'row_0'=8,'row_1'=4,'col'=2] {'row_0'}, dimensions={0} | all-to-all | bytes 1048576 | tf_op jit(solution)/shard_map/all_to_all | solution.py:220
  161.1 0.0 copy-start.1
  161.1 2.1 sums.1
  163.2 14.1 %all_to_all.49.refs_1_.refs_3_ = bf16[8,272,128]{2,1,0:T(8,128)(2,1)S(1)} all-to-all(bf16[8,272,128]{2,1,0:T(8,128)(2,1)} %sums.1), channel_id=1, replica_groups=mesh['freq'=4,'row_0'=8,'row_1'=4,'col'=2] {'row_1','col'}, dimensions={0} | all-to-all | bytes 1114112 | tf_op jit(solution)/shard_map/all_to_all | solution.py:220
  177.4 0.0 copy-done.3
  177.4 0.0 copy-done.1
  177.4 4.1 %gram.1 = (bf16[4,8,8,32,128]{4,3,2,1,0:T(8,128)(2,1)S(1)}, bf16[2,128,128]{2,1,0:T(8,128)(2,1)S(1)}) custom-call(s32[1]{0:T(128)} %bitcast.col_id.refs_0_, bf16[8,272,128]{2,1,0:T(8,128)(2,1)S(1)} %all_to_all.49.refs_1_.refs_3_, bf16[8,272,128]{2,1,0:T(8,128)(2,1)S(1)} %all-to-all-done.1.rows_ref.mask_ref.refs_2_, ...), custom_call_target="tpu_custom_call" | custom-call | tf_op jit(solution)/shard_map/gram/pallas_call | solution.py:305
  181.5 0.0 copy-start.2
  181.5 1.3 copy-done.2
  182.8 5.6 %all-to-all-start.8 = ((bf16[16,2,8,32,128]{4,3,2,1,0:T(8,128)(2,1)}), bf16[16,2,8,32,128]{4,3,2,1,0:T(8,128)(2,1)}, u32[]{:S(2)}, u32[]{:S(2)}) async-start(bf16[16,2,8,32,128]{4,3,2,1,0:T(8,128)(2,1)} %bitcast.34), calls=%async_computation.8 | async-start | bytes 4194304 | tf_op jit(solution)/shard_map/all_to_all | solution.py:220
  188.4 0.7 copy.30
  189.1 29.4 %all-to-all-done.8 = bf16[16,2,8,32,128]{4,3,2,1,0:T(8,128)(2,1)} async-done(((bf16[16,2,8,32,128]{4,3,2,1,0:T(8,128)(2,1)}), bf16[16,2,8,32,128]{4,3,2,1,0:T(8,128)(2,1)}, u32[]{:S(2)}, u32[]{:S(2)}) %all-to-all-start.8) | async-done | bytes 2097184 | tf_op jit(solution)/shard_map/all_to_all | solution.py:220
  218.6 2.0 convert_reduce_fusion
  220.6 1.0 copy.29
  (4 shorter events, 0.0 us)
Async XLA Ops:
  0.6 1.2 copy-start
  2.1 17.7 %copy-start.4 = (bf16[128,2,128]{2,1,0:T(2,128)(2,1)S(1)}, bf16[128,2,128]{2,1,0:T(2,128)(2,1)}, u32[]{:S(2)}) copy-start(bf16[128,2,128]{2,1,0:T(2,128)(2,1)} %param.6) | copy-start | bytes 196612
  3.9 9.9 %all-to-all-start = ((bf16[4,2,32,128]{3,2,1,0:T(8,128)(2,1)}), bf16[4,2,32,128]{3,2,1,0:T(8,128)(2,1)S(1)}, u32[]{:S(2)}, u32[]{:S(2)}) async-start(bf16[4,2,32,128]{3,2,1,0:T(8,128)(2,1)} %reshape.145), calls=%async_computation | async-start | bytes 131072 | tf_op jit(solution)/shard_map/all_to_all | solution.py:220
  14.9 14.1 %all-to-all-start.1 = ((bf16[8,272,128]{2,1,0:T(8,128)(2,1)}), bf16[8,272,128]{2,1,0:T(8,128)(2,1)S(1)}, u32[]{:S(2)}, u32[]{:S(2)}) async-start(bf16[8,272,128]{2,1,0:T(8,128)(2,1)} %pad_maximum_fusion), calls=%async_computation.1 | async-start | bytes 1114112 | tf_op jit(solution)/shard_map/all_to_all | solution.py:220
  30.2 36.9 %all-to-all-start.2 = ((bf16[8,512,128]{2,1,0:T(8,128)(2,1)}), bf16[8,512,128]{2,1,0:T(8,128)(2,1)S(1)}, u32[]{:S(2)}, u32[]{:S(2)}) async-start(bf16[8,512,128]{2,1,0:T(8,128)(2,1)} %broadcast_in_dim.21), calls=%async_computation.2 | async-start | bytes 2097152 | tf_op jit(solution)/shard_map/all_to_all | solution.py:220
  139.0 38.4 %copy-start.3 = (f32[256,128]{1,0:T(8,128)S(1)}, f32[256,128]{1,0:T(8,128)}, u32[]{:S(2)}) copy-start(f32[256,128]{1,0:T(8,128)} %get-tuple-element.15.scaled_ref.refs_5_) | copy-start | bytes 393220
  161.1 16.2 %copy-start.1 = (bf16[8,256,128]{2,1,0:T(8,128)(2,1)S(1)}, bf16[8,256,128]{2,1,0:T(8,128)(2,1)}, u32[]{:S(2)}) copy-start(bf16[8,256,128]{2,1,0:T(8,128)(2,1)} %all_to_all.48.cols_ref.refs_4_) | copy-start | bytes 1572868
  181.5 1.3 copy-start.2
  182.8 35.7 %all-to-all-start.8 = ((bf16[16,2,8,32,128]{4,3,2,1,0:T(8,128)(2,1)}), bf16[16,2,8,32,128]{4,3,2,1,0:T(8,128)(2,1)}, u32[]{:S(2)}, u32[]{:S(2)}) async-start(bf16[16,2,8,32,128]{4,3,2,1,0:T(8,128)(2,1)} %bitcast.34), calls=%async_computation.8 | async-start | bytes 4194304 | tf_op jit(solution)/shard_map/all_to_all | solution.py:220

commit v2 on v1

--- a/solution.py
+++ b/solution.py
@@ -212,6 +212,15 @@
             out_ref[x, 0, z] = value[x * 32 : (x + 1) * 32]
 
 
+def final_sum(tiles_ref, out_ref):
+    for y in range(4):
+        for z in range(Z // 2):
+            total = tiles_ref[0, y, 0, z].astype(F32)
+            for x in range(1, 4):
+                total = total + tiles_ref[x, y, 0, z].astype(F32)
+            out_ref[0, z, y] = total
+
+
 def whole(shape):
     return pl.BlockSpec(shape, lambda *_: (0,) * len(shape))
 
@@ -247,7 +256,8 @@
 
     row_spec = pl.BlockSpec((1, FREQ_DEV * BLK, BLK), lambda i, c: (i, 0, 0))
     mask_spec = pl.BlockSpec((1, EXTRA, BLK), lambda i, c: (i // 2 * 2 + c[0], 16, 0))
-    big = pltpu.CompilerParams(vmem_limit_bytes=48 << 20)
+    big = pltpu.CompilerParams(vmem_limit_bytes=16 << 20)
+    small = pltpu.CompilerParams(vmem_limit_bytes=6 << 20)
     stack = pltpu.VMEM((FREQ_DEV, 2 * SPAN, BLK), BF16)
     msg_shape = jax.ShapeDtypeStruct((YC, MSG, BLK), BF16)
     kernels, partial = pl.pallas_call(
@@ -274,6 +284,7 @@
             jax.ShapeDtypeStruct((Z, *own_shape), BF16),
             jax.ShapeDtypeStruct(own_shape, F32),
         ],
+        compiler_params=small,
         name="combine_one",
     )(got)
     cols = exchange(to_z, "row_0")
@@ -297,10 +308,13 @@
             jax.ShapeDtypeStruct(own_shape, F32),
             jax.ShapeDtypeStruct((Z, *own_shape), BF16),
         ],
+        compiler_params=small,
         name="combine_two",
     )(got, inverse)
     cols = exchange(to_z, "row_0")
-    to_yc = pl.pallas_call(sums_message, out_shape=msg_shape, name="sums")(cols, scaled)
+    to_yc = pl.pallas_call(
+        sums_message, out_shape=msg_shape, compiler_params=small, name="sums"
+    )(cols, scaled)
     last_rows = exchange(to_yc, YCOL)
     tiles, vectors = pl.pallas_call(
         lambda *refs: gram_kernel(*refs, images=images, freqs=freq_total),
@@ -326,11 +340,19 @@
         compiler_params=big,
         name="gram",
     )(col_id, last_rows, rows, last_rows, cols, scaled)
+    arrived = exchange(tiles.reshape(16, 2, Z, 32, BLK), ("freq", "row_1"))
+    arrived, vectors = lax.optimization_barrier((arrived, vectors))
     vectors = jnp.transpose(vectors, (1, 0, 2))
-    arrived = exchange(tiles.reshape(16, 2, Z, 32, BLK), ("freq", "row_1"))
-    summed = jnp.sum(arrived.reshape(4, 4, 2, Z, 32, BLK).astype(F32), axis=0)
-    affinity = jnp.transpose(summed, (1, 2, 0, 3, 4)).reshape(2, 32, 1, 1, 32, BLK)
-    return (vectors, affinity)
+    affinity = pl.pallas_call(
+        final_sum,
+        grid=(2, 2),
+        in_specs=[pl.BlockSpec((4, 4, 1, Z // 2, 32, BLK), lambda t, h: (0, 0, t, h, 0, 0))],
+        out_specs=pl.BlockSpec((1, Z // 2, 4, 32, BLK), lambda t, h: (t, h, 0, 0, 0)),
+        out_shape=jax.ShapeDtypeStruct((2, Z, 4, 32, BLK), F32),
+        compiler_params=small,
+        name="final",
+    )(arrived.reshape(4, 4, 2, Z, 32, BLK))
+    return (vectors, affinity.reshape(2, 32, 1, 1, 32, BLK))
 
 
 def solution(mesh):

time: 223 us -> 201 us (0.901)
  waiting for transfers between devices: 71.8 us -> 42.4 us
  blocking collectives: 85.2 us -> 111 us
  Pallas kernels: 29.2 us -> 20.7 us
  starting transfers between devices: 23.3 us -> 17.7 us
  local copies, waits for them, and re-layouts: 6.54 us -> 4.19 us
    all_to_all x4 -> x3, waiting for transfers between devices: 71.8 us -> 42.4 us  [exchange(): return lax.all_to_all(pieces, axes, 0, 0, tiled=True)]
    all_to_all x5 -> x6, blocking collectives: 85.2 us -> 111 us  [exchange(): return lax.all_to_all(pieces, axes, 0, 0, tiled=True)]
    all_to_all x4 -> x3, starting transfers between devices: 23.3 us -> 17.7 us  [exchange(): return lax.all_to_all(pieces, axes, 0, 0, tiled=True)]
    pallas_call x1, Pallas kernels: 7.57 us -> 3.72 us  [body(): pl.pallas_call(product_kernel, grid=(YC,), in_specs=[pl.BlockSpec((1, FRE...]
  transfers between devices with their start and end apart: 4 -> 3, of which waited for: 4 -> 3; matrix products, arithmetic and copies ran while one was open for 1% -> 0% of each run, Pallas kernels for 0% -> 0%
where the time goes in v2:
time: 201 us; the launch traced here: 199 us
  blocking collectives  111 us (55%)
  waiting for transfers between devices  42.4 us (21%)
  Pallas kernels  20.7 us (10%)
  starting transfers between devices  17.7 us (9%)
  local copies, waits for them, and re-layouts  4.19 us (2%)
    all_to_all x6, blocking collectives, exchange(): return lax.all_to_all(pieces, axes, 0, 0, tiled=True)  111 us
    all_to_all x3, waiting for transfers between devices, exchange(): return lax.all_to_all(pieces, axes, 0, 0, tiled=True)  42.4 us
    all_to_all x3, starting transfers between devices, exchange(): return lax.all_to_all(pieces, axes, 0, 0, tiled=True)  17.7 us
    pallas_call x1, Pallas kernels, body(): pl.pallas_call(cross_kernel, grid_spec=pltpu.PrefetchScalarGridSpec(num_s...  10.7 us
    pallas_call x1, Pallas kernels, body(): pl.pallas_call(lambda *refs: gram_kernel(*refs, images=images, freqs=freq...  4.13 us
  transfers between devices with their start and end apart: 3, of which 3 were waited for; matrix products, arithmetic and copies ran while one was open for 0% of the time, Pallas kernels for 0%

profile of v2, /device:TPU:8, one launch (start us, length us, event | category | flops | bytes accessed | tf_op | source)
XLA Modules:
  0.0 199.4 jit_solution(7547804744034555518)
XLA Ops:
  0.6 0.0 copy-start
  0.7 0.1 multiply_convert_fusion.1
  0.8 1.1 copy-done
  1.9 0.2 convolution_convert_fusion
  2.1 0.0 copy-start.1
  2.1 0.9 fusion
  3.0 0.1 copy.15
  3.2 0.7 reshape.145
  3.9 4.3 %all-to-all-start = ((bf16[4,2,32,128]{3,2,1,0:T(8,128)(2,1)}), bf16[4,2,32,128]{3,2,1,0:T(8,128)(2,1)S(1)}, u32[]{:S(2)}, u32[]{:S(2)}) async-start(bf16[4,2,32,128]{3,2,1,0:T(8,128)(2,1)} %reshape.145), calls=%async_computation | async-start | bytes 131072 | tf_op jit(solution)/shard_map/all_to_all | solution.py:229
  8.2 0.7 convert_reduce_fusion
  8.9 0.1 convert_element_type.49
  9.0 0.1 copy.23
  9.1 4.7 %all-to-all-done = bf16[4,2,32,128]{3,2,1,0:T(8,128)(2,1)S(1)} async-done(((bf16[4,2,32,128]{3,2,1,0:T(8,128)(2,1)}), bf16[4,2,32,128]{3,2,1,0:T(8,128)(2,1)S(1)}, u32[]{:S(2)}, u32[]{:S(2)}) %all-to-all-start) | async-done | bytes 65568 | tf_op jit(solution)/shard_map/all_to_all | solution.py:229
  13.9 0.1 copy.16
  13.9 0.1 broadcast_in_dim.20
  14.0 0.1 broadcast_in_dim.17
  14.1 0.8 pad_maximum_fusion
  14.9 4.9 %all-to-all-start.1 = ((bf16[8,272,128]{2,1,0:T(8,128)(2,1)}), bf16[8,272,128]{2,1,0:T(8,128)(2,1)S(1)}, u32[]{:S(2)}, u32[]{:S(2)}) async-start(bf16[8,272,128]{2,1,0:T(8,128)(2,1)} %pad_maximum_fusion), calls=%async_computation.1 | async-start | bytes 1114112 | tf_op jit(solution)/shard_map/all_to_all | solution.py:229
  19.8 0.0 copy-done.1
  19.9 9.2 %all-to-all-done.1.rows_ref.mask_ref.refs_2_ = bf16[8,272,128]{2,1,0:T(8,128)(2,1)S(1)} async-done(((bf16[8,272,128]{2,1,0:T(8,128)(2,1)}), bf16[8,272,128]{2,1,0:T(8,128)(2,1)S(1)}, u32[]{:S(2)}, u32[]{:S(2)}) %all-to-all-start.1) | async-done | bytes 557088 | tf_op jit(solution)/shard_map/all_to_all | solution.py:229
  29.1 1.1 broadcast_in_dim.21
  30.2 8.5 %all-to-all-start.2 = ((bf16[8,512,128]{2,1,0:T(8,128)(2,1)}), bf16[8,512,128]{2,1,0:T(8,128)(2,1)S(1)}, u32[]{:S(2)}, u32[]{:S(2)}) async-start(bf16[8,512,128]{2,1,0:T(8,128)(2,1)} %broadcast_in_dim.21), calls=%async_computation.2 | async-start | bytes 2097152 | tf_op jit(solution)/shard_map/all_to_all | solution.py:229
  38.6 28.4 %all-to-all-done.2.cols_ref = bf16[8,512,128]{2,1,0:T(8,128)(2,1)S(1)} async-done(((bf16[8,512,128]{2,1,0:T(8,128)(2,1)}), bf16[8,512,128]{2,1,0:T(8,128)(2,1)S(1)}, u32[]{:S(2)}, u32[]{:S(2)}) %all-to-all-start.2) | async-done | bytes 1048608 | tf_op jit(solution)/shard_map/all_to_all | solution.py:229
  67.1 10.7 %cross.1 = (bf16[8,2,128,2048]{3,2,1,0:T(8,128)(2,1)S(1)}, bf16[8,272,128]{2,1,0:T(8,128)(2,1)S(1)}) custom-call(s32[1]{0:T(128)} %bitcast.col_id.refs_0_, bf16[8,272,128]{2,1,0:T(8,128)(2,1)S(1)} %all-to-all-done.1.rows_ref.mask_ref.refs_2_, bf16[8,272,128]{2,1,0:T(8,128)(2,1)S(1)} %all-to-all-done.1.rows_ref.mask_ref.refs_2_, ...), custom_call_target="tpu_custom_call" | custom-call | tf_op jit(solution)/shard_map/cross/pallas_call | solution.py:263
  77.8 13.1 %all_to_all.45.recv_ref = bf16[8,272,128]{2,1,0:T(8,128)(2,1)S(1)} all-to-all(bf16[8,272,128]{2,1,0:T(8,128)(2,1)S(1)} %get-tuple-element.13), channel_id=1, replica_groups=mesh['freq'=4,'row_0'=8,'row_1'=4,'col'=2] {'row_1','col'}, dimensions={0} | all-to-all | bytes 1114112 | tf_op jit(solution)/shard_map/all_to_all | solution.py:229
  90.9 0.1 combine_one.1
  91.0 20.3 %all_to_all.46.cols_ref = bf16[8,256,128]{2,1,0:T(8,128)(2,1)S(1)} all-to-all(bf16[8,256,128]{2,1,0:T(8,128)(2,1)S(1)} %get-tuple-element.14), channel_id=1, replica_groups=mesh['freq'=4,'row_0'=8,'row_1'=4,'col'=2] {'row_0'}, dimensions={0} | all-to-all | bytes 1048576 | tf_op jit(solution)/shard_map/all_to_all | solution.py:229
  111.3 3.7 %product.1 = bf16[8,272,128]{2,1,0:T(8,128)(2,1)S(1)} custom-call(bf16[8,2,128,2048]{3,2,1,0:T(8,128)(2,1)S(1)} %get-tuple-element.12.kern_ref, bf16[8,256,128]{2,1,0:T(8,128)(2,1)S(1)} %all_to_all.46.cols_ref), custom_call_target="tpu_custom_call" | custom-call | tf_op jit(solution)/shard_map/product/pallas_call | solution.py:291
  115.1 13.1 %all_to_all.47.refs_0_ = bf16[8,272,128]{2,1,0:T(8,128)(2,1)S(1)} all-to-all(bf16[8,272,128]{2,1,0:T(8,128)(2,1)S(1)} %product.1), channel_id=1, replica_groups=mesh['freq'=4,'row_0'=8,'row_1'=4,'col'=2] {'row_1','col'}, dimensions={0} | all-to-all | bytes 1114112 | tf_op jit(solution)/shard_map/all_to_all | solution.py:229
  128.2 0.1 combine_two.1
  128.2 20.3 %all_to_all.48.cols_ref.refs_4_ = bf16[8,256,128]{2,1,0:T(8,128)(2,1)S(1)} all-to-all(bf16[8,256,128]{2,1,0:T(8,128)(2,1)S(1)} %get-tuple-element.16), channel_id=1, replica_groups=mesh['freq'=4,'row_0'=8,'row_1'=4,'col'=2] {'row_0'}, dimensions={0} | all-to-all | bytes 1048576 | tf_op jit(solution)/shard_map/all_to_all | solution.py:229
  148.5 0.2 sums.1
  148.7 13.1 %all_to_all.49.refs_1_.refs_3_ = bf16[8,272,128]{2,1,0:T(8,128)(2,1)S(1)} all-to-all(bf16[8,272,128]{2,1,0:T(8,128)(2,1)S(1)} %sums.1), channel_id=1, replica_groups=mesh['freq'=4,'row_0'=8,'row_1'=4,'col'=2] {'row_1','col'}, dimensions={0} | all-to-all | bytes 1114112 | tf_op jit(solution)/shard_map/all_to_all | solution.py:229
  161.8 4.1 %gram.1 = (bf16[4,8,8,32,128]{4,3,2,1,0:T(8,128)(2,1)S(1)}, bf16[2,128,128]{2,1,0:T(8,128)(2,1)S(1)}) custom-call(s32[1]{0:T(128)} %bitcast.col_id.refs_0_, bf16[8,272,128]{2,1,0:T(8,128)(2,1)S(1)} %all_to_all.49.refs_1_.refs_3_, bf16[8,272,128]{2,1,0:T(8,128)(2,1)S(1)} %all-to-all-done.1.rows_ref.mask_ref.refs_2_, ...), custom_call_target="tpu_custom_call" | custom-call | tf_op jit(solution)/shard_map/gram/pallas_call | solution.py:319
  165.9 31.0 %all_to_all.50 = bf16[16,2,8,32,128]{4,3,2,1,0:T(8,128)(2,1)S(1)} all-to-all(bf16[16,2,8,32,128]{4,3,2,1,0:T(8,128)(2,1)S(1)} %bitcast.33), channel_id=1, replica_groups=mesh['freq'=4,'row_0'=8,'row_1'=4,'col'=2] {'freq','row_1'}, dimensions={0} | all-to-all | bytes 4194304 | tf_op jit(solution)/shard_map/all_to_all | solution.py:229
  196.9 0.7 copy.19
  197.6 1.7 final.1
  (4 shorter events, 0.0 us)
Async XLA Ops:
  0.6 1.2 copy-start
  2.1 17.7 %copy-start.1 = (bf16[128,2,128]{2,1,0:T(2,128)(2,1)S(1)}, bf16[128,2,128]{2,1,0:T(2,128)(2,1)}, u32[]{:S(2)}) copy-start(bf16[128,2,128]{2,1,0:T(2,128)(2,1)} %param.6) | copy-start | bytes 196612
  3.9 9.9 %all-to-all-start = ((bf16[4,2,32,128]{3,2,1,0:T(8,128)(2,1)}), bf16[4,2,32,128]{3,2,1,0:T(8,128)(2,1)S(1)}, u32[]{:S(2)}, u32[]{:S(2)}) async-start(bf16[4,2,32,128]{3,2,1,0:T(8,128)(2,1)} %reshape.145), calls=%async_computation | async-start | bytes 131072 | tf_op jit(solution)/shard_map/all_to_all | solution.py:229
  14.9 14.1 %all-to-all-start.1 = ((bf16[8,272,128]{2,1,0:T(8,128)(2,1)}), bf16[8,272,128]{2,1,0:T(8,128)(2,1)S(1)}, u32[]{:S(2)}, u32[]{:S(2)}) async-start(bf16[8,272,128]{2,1,0:T(8,128)(2,1)} %pad_maximum_fusion), calls=%async_computation.1 | async-start | bytes 1114112 | tf_op jit(solution)/shard_map/all_to_all | solution.py:229
  30.2 36.9 %all-to-all-start.2 = ((bf16[8,512,128]{2,1,0:T(8,128)(2,1)}), bf16[8,512,128]{2,1,0:T(8,128)(2,1)S(1)}, u32[]{:S(2)}, u32[]{:S(2)}) async-start(bf16[8,512,128]{2,1,0:T(8,128)(2,1)} %broadcast_in_dim.21), calls=%async_computation.2 | async-start | bytes 2097152 | tf_op jit(solution)/shard_map/all_to_all | solution.py:229
